TPU v7x, 32 devices: a whole 2x2x4 slice. The times are simulated.
32 devices in a mesh: grp: 2 (over x), seq: 16 (over z, y, core).
Axes of the slice: x: 2, y: 2, z: 4, core: 2. Of those that a mesh axis runs over, the one named last changes fastest.
Arguments:
- alignment: bfloat16 [64, 128, 768], P(('grp', 'seq')), parts along dimension 0, may hold values from -20 to 20
- protein_id: int32 [256], P('grp'), parts along dimension 0, may hold values from 0 to 3, never falling along the last dimension, each value on 1 to 64 neighbouring positions
- row_depth: int32 [8], P('grp'), parts along dimension 0, may hold values from 8 to 32, as said below
- row_gain: float32 [768], replicated, may hold values from 0.1 to 1.9
- row_query: bfloat16 [768, 768], replicated, may hold values from -40 to 40
- row_key: bfloat16 [768, 768], replicated, may hold values from -0.21875 to 0.21875
- row_value: bfloat16 [768, 768], replicated, may hold values from -0.21875 to 0.21875
- row_output: bfloat16 [768, 768], replicated, may hold values from -0.21875 to 0.21875
- column_gain: float32 [768], replicated, may hold values from 0.1 to 1.9
- column_query: bfloat16 [768, 768], replicated, may hold values from -40 to 40
- column_key: bfloat16 [768, 768], replicated, may hold values from -0.21875 to 0.21875
- column_value: bfloat16 [768, 768], replicated, may hold values from -0.21875 to 0.21875
- column_output: bfloat16 [768, 768], replicated, may hold values from -0.21875 to 0.21875
Outputs:
- layer_out: bfloat16 [64, 128, 768], P(('grp', 'seq')), parts along dimension 0
There are 2 independent parts, one for each index of `grp`. A program takes and returns all parts, laid end to end along the dimension named above; an argument that names none is the same for every part. Nothing has to cross between parts.
Inputs may be any that keep to these rules, and one draw needn't show every extreme that they name: `row_depth`: row 0 is real for every protein; one protein of each pack has all 32 rows real. `protein_id`: proteins occupy contiguous column ranges in order, each 1 to 64 columns.
All inputs are finite; a program needn't handle non-finite values.
Results may differ from a plain program's by a relative error of at most 0.011.
Values may be sent and summed in bfloat16 or wider, within the bound.
No kernel may reach another device: no remote copies, remote signals or barrier semaphores. Data moves between devices by JAX's collectives and lax.ppermute only.
A program may use at most 64 MiB of HBM per device.

v0:
```python
import math
import jax
import jax.numpy as jnp
from jax import lax
from jax.sharding import PartitionSpec as P

H = 12


def layer_norm(values, gain):
    full = values.astype(jnp.float32)
    middle = jnp.mean(full, axis=-1, keepdims=True)
    spread = jnp.mean((full - middle) ** 2, axis=-1, keepdims=True)
    return ((full - middle) * lax.rsqrt(spread + 1e-05) * gain).astype(jnp.bfloat16)


def project(normed, weight):
    shape = normed.shape
    flattened = normed.reshape(-1, shape[-1])
    return (
        jnp.dot(flattened, weight, preferred_element_type=jnp.float32)
        .astype(jnp.bfloat16)
        .reshape(shape[:-1] + (weight.shape[1],))
    )


def column_depth(protein_id, row_depth):
    onehot = protein_id[:, None] == jnp.arange(row_depth.shape[0], dtype=jnp.int32)[None, :]
    return jnp.sum(jnp.where(onehot, row_depth[None, :], 0), axis=1)


def per_device(
    alignment,
    protein_id,
    row_depth,
    row_gain,
    row_query,
    row_key,
    row_value,
    row_output,
    column_gain,
    column_query,
    column_key,
    column_value,
    column_output,
):
    rows_dev, columns, width = alignment.shape
    devices = lax.axis_size("seq")
    position = lax.axis_index("seq")
    total_rows = rows_dev * devices
    head_count = H
    head_size = width // head_count
    tile_cols = columns // devices
    depth_col = column_depth(protein_id, row_depth)
    row_ids = position * rows_dev + jnp.arange(rows_dev, dtype=jnp.int32)
    valid = row_ids[:, None] < depth_col[None, :]
    mask_bf = valid.astype(jnp.bfloat16)[:, :, None]
    normed_row = layer_norm(alignment, row_gain)
    query_a = (project(normed_row, row_query) * mask_bf).reshape(
        rows_dev, columns, head_count, head_size
    )
    key_a = (project(normed_row, row_key) * mask_bf).reshape(
        rows_dev, columns, head_count, head_size
    )
    value_a = project(normed_row, row_value).reshape(rows_dev, columns, head_count, head_size)
    scale = 1.0 / (math.sqrt(head_size) * math.sqrt(total_rows))
    tied = (
        lax.psum_scatter(
            jnp.einsum("rihe,rjhe->ihj", query_a, key_a, preferred_element_type=jnp.float32),
            "seq",
            scatter_dimension=0,
            tiled=True,
        )
        * scale
    )
    prot_query = lax.dynamic_slice_in_dim(protein_id, position * tile_cols, tile_cols, 0)
    same_prot = prot_query[:, None, None] == protein_id[None, None, :]
    tied = jnp.where(same_prot, tied, -1000000000.0)
    row_weights = jax.nn.softmax(tied, axis=-1).astype(jnp.bfloat16)
    row_mixed = (
        jnp.einsum(
            "ihj,rjhe->rihe",
            lax.all_gather(row_weights, "seq", axis=0, tiled=True),
            value_a,
            preferred_element_type=jnp.float32,
        )
        .astype(jnp.bfloat16)
        .reshape(rows_dev, columns, width)
    )
    after_row = (
        alignment.astype(jnp.float32)
        + jnp.dot(
            row_mixed.reshape(-1, width), row_output, preferred_element_type=jnp.float32
        ).reshape(rows_dev, columns, width)
    ).astype(jnp.bfloat16)
    normed_col = layer_norm(after_row, column_gain)
    moved = lax.all_to_all(normed_col, "seq", split_axis=1, concat_axis=0, tiled=True)
    query_b = project(moved, column_query)
    key_b = project(moved, column_key)
    value_b = project(moved, column_value)
    query_b = query_b.reshape(total_rows, tile_cols, head_count, head_size)
    key_b = key_b.reshape(total_rows, tile_cols, head_count, head_size)
    value_b = value_b.reshape(total_rows, tile_cols, head_count, head_size)
    depth_tile = lax.dynamic_slice_in_dim(depth_col, position * tile_cols, tile_cols, 0)
    key_valid = jnp.arange(total_rows, dtype=jnp.int32)[None, :] < depth_tile[:, None]
    col_scores = jnp.einsum(
        "rche,sche->chrs", query_b, key_b, preferred_element_type=jnp.float32
    ) / math.sqrt(head_size)
    col_scores = jnp.where(key_valid[:, None, None, :], col_scores, -1000000000.0)
    col_weights = jax.nn.softmax(col_scores, axis=-1).astype(jnp.bfloat16)
    col_mixed = jnp.einsum(
        "chrs,sche->rche", col_weights, value_b, preferred_element_type=jnp.float32
    ).astype(jnp.bfloat16)
    col_mixed = col_mixed.reshape(total_rows, tile_cols, width)
    returned = lax.all_to_all(col_mixed, "seq", split_axis=0, concat_axis=1, tiled=True)
    layer_out = after_row.astype(jnp.float32) + jnp.dot(
        returned.reshape(-1, width), column_output, preferred_element_type=jnp.float32
    ).reshape(rows_dev, columns, width)
    return layer_out.astype(jnp.bfloat16)


def solution(mesh):
    return jax.shard_map(
        per_device,
        mesh=mesh,
        in_specs=(
            P(("grp", "seq"), None, None),
            P("grp"),
            P("grp"),
            P(),
            P(),
            P(),
            P(),
            P(),
            P(),
            P(),
            P(),
            P(),
            P(),
        ),
        out_specs=P(("grp", "seq"), None, None),
        check_vma=False,
    )
```

profile of v0, /device:TPU:0, one launch (start us, length us, event | category | flops | bytes accessed | tf_op | source)
XLA Modules:
  0.0 158.1 jit_solution(10954076205752719301)
XLA Ops:
  6.5 1.3 convert_reduce_fusion
  7.8 1.2 fusion.15
  9.1 1.2 fusion.17
  10.3 0.5 convolution_convert_fusion.5
  10.8 0.2 copy.75
  11.0 0.1 reshape.141
  11.1 1.7 %convolution_convert_fusion.4 = bf16[256,768]{1,0:T(8,128)(2,1)S(1)} fusion(bf16[256,768]{1,0:T(8,128)(2,1)S(1)} %bitcast.61, bf16[768,768]{1,0:T(8,128)(2,1)} %param.17), kind=kOutput, calls=%fused_computation.17 | convolution fusion | flops 302186496 | bytes 1966080 | tf_op jit(solution)/shard_map/dot_general | solution.py:21
  12.9 0.2 copy.76
  13.0 0.1 reshape.142
  13.2 0.3 copy-done.6
  13.5 0.0 copy-done.7
  13.5 0.1 select_reduce_fusion
  13.6 0.1 compare_convert_fusion
  13.7 0.1 broadcast_multiply_fusion.1
  13.7 0.3 convolution_bitcast_fusion
  14.1 0.0 copy-start.3
  14.1 1.4 copy.79
  15.5 0.0 reduce-scatter.2.cloned.1.call-update
  15.5 0.1 dynamic_slice.6
  15.6 0.5 convolution_convert_fusion.6
  16.1 0.2 copy.74
  16.2 0.1 reshape_reshape.13
  16.3 0.1 broadcast_compare_fusion
  16.4 59.4 %reduce-scatter.2.cloned.1.call-done = f32[8,12,128]{2,1,0:T(8,128)} async-done(((f32[128,12,128]{2,1,0:T(8,128)}), f32[8,12,128]{2,1,0:T(8,128)}) %reduce-scatter.2.cloned.1.call-update) | async-done | bytes 49168 | tf_op jit(solution)/shard_map/reduce_scatter | solution.py:68
  75.8 1.0 fusion.38
  76.8 0.1 divide_convert_fusion.2
  76.9 20.5 %all_gather.3 = bf16[128,12,128]{2,0,1:T(8,128)(2,1)S(1)} all-gather(bf16[8,12,128]{2,0,1:T(8,128)(2,1)S(1)} %copy.80), channel_id=1, replica_groups=mesh['grp'=2,'seq'=16] {'seq'}, dimensions={0}, use_global_device_ids=true | all-gather | bytes 417792 | tf_op jit(solution)/shard_map/all_gather | solution.py:83
  97.5 0.4 fusion.8
  97.9 0.6 fusion.39
  98.5 0.2 multiply_reduce_fusion
  98.8 0.2 multiply_convert_fusion
  99.0 1.2 copy.84
  100.1 3.6 %all-to-all-start = ((bf16[2,128,768]{2,0,1:T(2,128)(2,1)}), bf16[2,128,768]{2,0,1:T(2,128)(2,1)S(1)}, u32[]{:S(2)}, u32[]{:S(2)}) async-start(bf16[2,128,768]{2,0,1:T(2,128)(2,1)} %copy.84), calls=%async_computation.1 | async-start | bytes 786432 | tf_op jit(solution)/shard_map/all_to_all | solution.py:97
  103.7 0.1 dynamic_slice.7
  103.7 0.1 iota_compare_fusion
  103.8 12.0 %all-to-all-done = bf16[2,128,768]{2,0,1:T(2,128)(2,1)S(1)} async-done(((bf16[2,128,768]{2,0,1:T(2,128)(2,1)}), bf16[2,128,768]{2,0,1:T(2,128)(2,1)S(1)}, u32[]{:S(2)}, u32[]{:S(2)}) %all-to-all-start) | async-done | bytes 393248 | tf_op jit(solution)/shard_map/all_to_all | solution.py:97
  115.9 1.7 %convolution_convert_fusion.2 = bf16[256,768]{1,0:T(8,128)(2,1)S(1)} fusion(bf16[256,768]{1,0:T(8,128)(2,1)S(1)} %bitcast.63, bf16[768,768]{1,0:T(8,128)(2,1)} %param.22), kind=kOutput, calls=%fused_computation.15 | convolution fusion | flops 302186496 | bytes 1966080 | tf_op jit(solution)/shard_map/dot_general | solution.py:21
  117.7 1.6 %reshape_reshape.15 = bf16[32,8,12,64]{3,2,1,0:T(8,128)(2,1)} reshape(bf16[256,768]{1,0:T(8,128)(2,1)S(1)} %convolution_convert_fusion.2) | data formatting | bytes 786432 | tf_op jit(solution)/shard_map/reshape;reshape | solution.py:101
  119.3 1.7 %convolution_convert_fusion.1 = bf16[256,768]{1,0:T(8,128)(2,1)S(1)} fusion(bf16[256,768]{1,0:T(8,128)(2,1)S(1)} %bitcast.64, bf16[768,768]{1,0:T(8,128)(2,1)} %param.23), kind=kOutput, calls=%fused_computation.14 | convolution fusion | flops 302186496 | bytes 1966080 | tf_op jit(solution)/shard_map/dot_general | solution.py:21
  121.0 1.6 reshape_reshape.16
  122.6 1.7 %convolution_convert_fusion.3 = bf16[256,768]{1,0:T(8,128)(2,1)S(1)} fusion(bf16[256,768]{1,0:T(8,128)(2,1)S(1)} %bitcast.65, bf16[768,768]{1,0:T(8,128)(2,1)} %param.24), kind=kOutput, calls=%fused_computation.16 | convolution fusion | flops 302186496 | bytes 1966080 | tf_op jit(solution)/shard_map/dot_general | solution.py:21
  124.3 1.6 reshape_reshape.14
  125.9 4.2 %fusion.40 = (f32[8,12,32]{2,1,0:T(8,128)S(1)}, f32[8,12,32,32]{2,3,1,0:T(8,128)}) fusion(bf16[32,8,12,64]{3,2,1,0:T(8,128)(2,1)} %reshape_reshape.16, bf16[32,8,12,64]{3,2,1,0:T(8,128)(2,1)} %reshape_reshape.15, pred[8,32]{1,0:T(8,128)(4,1)S(1)} %iota_compare_fusion), kind=kOutput, calls=%fused_computation.68 | convolution fusion | flops 12976159 | bytes 1192192 | tf_op jit(solution)/shard_map/sub | solution.py:110
  130.1 2.1 %fusion.4 = bf16[32,8,12,64]{3,0,2,1:T(8,128)(2,1)S(1)} fusion(f32[8,12,32,32]{2,3,1,0:T(8,128)} %get-tuple-element.12, bf16[32,8,12,64]{3,2,1,0:T(8,128)(2,1)S(1)} %copy-done.4, f32[8,12,32]{2,1,0:T(8,128)S(1)} %get-tuple-element.11), kind=kOutput, calls=%fused_computation.7 | convolution fusion | flops 12976128 | bytes 1191936 | tf_op jit(solution)/shard_map/chrs,sche->rche/dot_general | solution.py:111
  132.3 0.3 copy.91
  132.6 0.6 reshape.144
  133.3 15.5 %all_to_all.30 = bf16[32,8,768]{2,1,0:T(8,128)(2,1)S(1)} all-to-all(bf16[32,8,768]{2,1,0:T(8,128)(2,1)S(1)} %reshape.144), channel_id=1, replica_groups=mesh['grp'=2,'seq'=16] {'seq'}, dimensions={0} | all-to-all | bytes 786432 | tf_op jit(solution)/shard_map/all_to_all | solution.py:115
  148.7 2.5 %fusion.7 = bf16[2,128,768]{2,1,0:T(8,128)(2,1)} fusion(f32[2,128,768]{2,1,0:T(8,128)S(1)} %get-tuple-element.10, bf16[768,768]{1,0:T(8,128)(2,1)} %param.25, bf16[2,16,8,768]{3,2,0,1:T(8,128)(2,1)S(1)} %bitcast.72), kind=kOutput, calls=%fused_computation.13 | convolution fusion | flops 302383104 | bytes 2752512 | tf_op jit(solution)/shard_map/dot_general | solution.py:116
  (24 shorter events, 0.2 us)
Async XLA Ops:
  6.5 91.4 %copy-start = (bf16[768,768]{1,0:T(8,128)(2,1)S(1)}, bf16[768,768]{1,0:T(8,128)(2,1)}, u32[]{:S(2)}) copy-start(bf16[768,768]{1,0:T(8,128)(2,1)} %param.20) | copy-start | bytes 3538948
  6.5 3.8 %copy-start.2 = (bf16[768,768]{1,0:T(8,128)(2,1)S(1)}, bf16[768,768]{1,0:T(8,128)(2,1)}, u32[]{:S(2)}) copy-start(bf16[768,768]{1,0:T(8,128)(2,1)} %param.18) | copy-start | bytes 3538948
  6.5 69.2 %reduce-scatter.2.cloned.1.call-start = ((), (), s32[]{:S(2)}) async-start(), calls=%async_computation.3 | async-start | bytes 1114112 | tf_op jit(solution)/shard_map/reduce_scatter | solution.py:68
  12.8 0.7 copy-start.6
  12.8 0.7 copy-start.7
  14.1 1.5 copy-start.3
  76.9 21.0 %copy-start.1 = (bf16[2,128,768]{2,1,0:T(8,128)(2,1)S(1)}, bf16[2,128,768]{2,1,0:T(8,128)(2,1)}, u32[]{:S(2)}) copy-start(bf16[2,128,768]{2,1,0:T(8,128)(2,1)} %param.13) | copy-start | bytes 1179652
  97.9 0.8 copy-start.5
  100.1 15.7 %all-to-all-start = ((bf16[2,128,768]{2,0,1:T(2,128)(2,1)}), bf16[2,128,768]{2,0,1:T(2,128)(2,1)S(1)}, u32[]{:S(2)}, u32[]{:S(2)}) async-start(bf16[2,128,768]{2,0,1:T(2,128)(2,1)} %copy.84), calls=%async_computation.1 | async-start | bytes 786432 | tf_op jit(solution)/shard_map/all_to_all | solution.py:97
  125.9 4.2 %copy-start.4 = (bf16[32,8,12,64]{3,2,1,0:T(8,128)(2,1)S(1)}, bf16[32,8,12,64]{3,2,1,0:T(8,128)(2,1)}, u32[]{:S(2)}) copy-start(bf16[32,8,12,64]{3,2,1,0:T(8,128)(2,1)} %reshape_reshape.14) | copy-start | bytes 1179652
Sparse Core Ops, SparseCore 0:
  15.6 60.1 reduce-scatter.1
where the time goes:
time: 159 us; the launch traced here: 158 us
  waiting for transfers between devices  71.4 us (45%)
  blocking collectives  36 us (23%)
  matrix products  18.1 us (11%)
  between operations  13.7 us (9%)
  local copies, waits for them, and re-layouts  9.7 us (6%)
  other arithmetic  5.64 us (4%)
  starting transfers between devices  3.56 us (2%)
    reduce_scatter x1, waiting for transfers between devices, per_device(): lax.psum_scatter(jnp.einsum('rihe,rjhe->ihj', query_a, key_a, preferred_e...  59.4 us
    all_gather x1, blocking collectives, per_device(): lax.all_gather(row_weights, 'seq', axis=0, tiled=True)  20.5 us
    all_to_all x1, blocking collectives, per_device(): lax.all_to_all(col_mixed, 'seq', split_axis=0, concat_axis=1, tiled=True)  15.5 us
    all_to_all x1, waiting for transfers between devices, per_device(): lax.all_to_all(normed_col, 'seq', split_axis=1, concat_axis=0, tiled=True)  12 us
    dot_general x6, matrix products, project(): jnp.dot(flattened, weight, preferred_element_type=jnp.float32)  7.94 us
    sub x1, matrix products, per_device(): col_weights = jax.nn.softmax(col_scores, axis=-1).astype(jnp.bfloat16)  4.24 us
    all_to_all x1, starting transfers between devices, per_device(): lax.all_to_all(normed_col, 'seq', split_axis=1, concat_axis=0, tiled=True)  3.55 us
  transfers between devices with their start and end apart: 2, of which 2 were waited for; matrix products, arithmetic and copies ran while one was open for 1% of the time, Pallas kernels for 0%

commit v1 on v0

--- a/solution.py
+++ b/solution.py
@@ -5,6 +5,15 @@
 from jax.sharding import PartitionSpec as P
 
 H = 12
+
+
+def _register_tables(x_in, dim_no):
+    x_in = jnp.moveaxis(x_in, 0, dim_no)
+    carry_in = x_in.shape
+    a_now = x_in.reshape(
+        *carry_in[:dim_no], carry_in[dim_no] * carry_in[dim_no + 1], *carry_in[dim_no + 2 :]
+    )
+    return a_now
 
 
 def layer_norm(values, gain):
@@ -77,10 +86,37 @@
     same_prot = prot_query[:, None, None] == protein_id[None, None, :]
     tied = jnp.where(same_prot, tied, -1000000000.0)
     row_weights = jax.nn.softmax(tied, axis=-1).astype(jnp.bfloat16)
+
+    def refer_column(patch, dimension_no, a_name):
+        n_peers_all = lax.axis_size(a_name)
+        bank = [(it, (it + 1) % n_peers_all) for it in range(n_peers_all)]
+        gallery = [(rr, ii) for ii, rr in bank]
+        local_out, arr_next = ([], [])
+        to_i = 0
+        while to_i < n_peers_all - 1:
+            if to_i % 2 == 0:
+                far_arr = lax.ppermute(
+                    local_out[-1] if local_out else patch, axis_name=a_name, perm=bank
+                )
+                local_out.append(far_arr)
+            else:
+                e_next = lax.ppermute(
+                    arr_next[-1] if arr_next else patch, axis_name=a_name, perm=gallery
+                )
+                arr_next.append(e_next)
+            to_i = to_i + 1
+        main = jnp.stack([*local_out[::-1], patch, *arr_next], axis=0)
+        arr_out = lax.axis_index(a_name)
+        inter = len(local_out)
+        right_arr = arr_out - inter
+        main = main[(jnp.arange(n_peers_all) - right_arr) % n_peers_all]
+        w2 = _register_tables(main, dimension_no)
+        return w2
+
     row_mixed = (
         jnp.einsum(
             "ihj,rjhe->rihe",
-            lax.all_gather(row_weights, "seq", axis=0, tiled=True),
+            refer_column(row_weights, 0, "seq"),
             value_a,
             preferred_element_type=jnp.float32,
         )

time: 159 us -> 190 us (1.19)
  starting transfers between devices: 3.56 us -> 37 us
  blocking collectives: 36 us -> 15.5 us
  waiting for transfers between devices: 71.4 us -> 88.8 us
    ppermute x0 -> x15, starting transfers between devices: none -> 31.2 us  [the longest x7 31.1 us: refer_column(): lax.ppermute(arr_next[-1] if arr_next else patch, axis_name=a_name, perm=...]
    all_gather x1 -> x0, blocking collectives: 20.5 us -> none  [per_device(): lax.all_gather(row_weights, 'seq', axis=0, tiled=True)]
    ppermute x0 -> x15, waiting for transfers between devices: none -> 16.6 us  [the longest x8 15.5 us: refer_column(): lax.ppermute(local_out[-1] if local_out else patch, axis_name=a_name, per...]
    all_to_all x1, starting transfers between devices: 3.55 us -> 5.83 us  [per_device(): lax.all_to_all(normed_col, 'seq', split_axis=1, concat_axis=0, tiled=True)]
  transfers between devices with their start and end apart: 2 -> 17, of which waited for: 2 -> 13; matrix products, arithmetic and copies ran while one was open for 1% -> 1% of each run, Pallas kernels for 0% -> 0%
where the time goes in v1:
time: 190 us
  waiting for transfers between devices  88.8 us (47%)
  starting transfers between devices  37 us (19%)
  matrix products  18.1 us (10%)
  blocking collectives  15.5 us (8%)
  between operations  13.8 us (7%)
  local copies, waits for them, and re-layouts  11.1 us (6%)
  other arithmetic  5.58 us (3%)
    reduce_scatter x1, waiting for transfers between devices, per_device(): lax.psum_scatter(jnp.einsum('rihe,rjhe->ihj', query_a, key_a, preferred_e...  60.1 us
    ppermute x7, starting transfers between devices, refer_column(): lax.ppermute(arr_next[-1] if arr_next else patch, axis_name=a_name, perm=...  31.1 us
    all_to_all x1, blocking collectives, per_device(): lax.all_to_all(col_mixed, 'seq', split_axis=0, concat_axis=1, tiled=True)  15.5 us
    ppermute x8, waiting for transfers between devices, refer_column(): lax.ppermute(local_out[-1] if local_out else patch, axis_name=a_name, per...  15.5 us
    all_to_all x1, waiting for transfers between devices, per_device(): lax.all_to_all(normed_col, 'seq', split_axis=1, concat_axis=0, tiled=True)  12 us
    dot_general x6, matrix products, project(): jnp.dot(flattened, weight, preferred_element_type=jnp.float32)  7.94 us
    all_to_all x1, starting transfers between devices, per_device(): lax.all_to_all(normed_col, 'seq', split_axis=1, concat_axis=0, tiled=True)  5.83 us
    sub x1, matrix products, per_device(): col_weights = jax.nn.softmax(col_scores, axis=-1).astype(jnp.bfloat16)  4.24 us
  transfers between devices with their start and end apart: 17, of which 13 were waited for; matrix products, arithmetic and copies ran while one was open for 1% of the time, Pallas kernels for 0%

profile of v1, /device:TPU:0, one launch (start us, length us, event | category | flops | bytes accessed | tf_op | source)
XLA Modules:
  0.0 189.9 jit_solution(8460997103363839832)
XLA Ops:
  6.5 1.3 convert_reduce_fusion
  7.8 1.2 fusion.18
  9.1 1.2 fusion.20
  10.3 0.5 convolution_convert_fusion.5
  11.1 1.7 convolution_convert_fusion.4
  13.2 0.3 copy-done.6
  13.7 0.3 convolution_bitcast_fusion
  14.1 1.4 copy.109
  15.6 60.1 %reduce-scatter.2.cloned.1.call-done = f32[8,12,128]{2,1,0:T(8,128)} async-done(((f32[128,12,128]{2,1,0:T(8,128)}), f32[8,12,128]{2,1,0:T(8,128)}) %reduce-scatter.2.cloned.1.call-update) | async-done | bytes 49168 | tf_op jit(solution)/shard_map/reduce_scatter | solution.py:77
  75.8 1.0 fusion.15
  76.9 6.0 %collective-permute-done = bf16[8,12,128]{2,1,0:T(8,128)(2,1)S(1)} collective-permute-done((bf16[8,12,128]{2,1,0:T(8,128)(2,1)S(1)}, bf16[8,12,128]{2,1,0:T(8,128)(2,1)S(1)}, u32[]{:S(2)}, u32[]{:S(2)}) %collective-permute-start) | collective-permute-done | bytes 24608 | tf_op jit(solution)/shard_map/ppermute | solution.py:98
  82.9 4.4 %collective-permute-start.8 = (bf16[8,12,128]{2,1,0:T(8,128)(2,1)S(1)}, bf16[8,12,128]{2,1,0:T(8,128)(2,1)S(1)}, u32[]{:S(2)}, u32[]{:S(2)}) collective-permute-start(bf16[8,12,128]{2,1,0:T(8,128)(2,1)S(1)} %fusion.15), channel_id=1, source_target_pairs={{1,0},{2,1},{3,2},{4,3},{5,4},{6,5},{7,6},{8,7},{9,8},{10,9},{11,1... | collective-permute-start | bytes 73736 | tf_op jit(solution)/shard_map/ppermute | solution.py:103
  87.3 1.6 collective-permute-done.1
  88.9 4.4 %collective-permute-start.9 = (bf16[8,12,128]{2,1,0:T(8,128)(2,1)S(1)}, bf16[8,12,128]{2,1,0:T(8,128)(2,1)S(1)}, u32[]{:S(2)}, u32[]{:S(2)}) collective-permute-start(bf16[8,12,128]{2,1,0:T(8,128)(2,1)S(1)} %collective-permute-done.8), channel_id=1, source_target_pairs={{1,0},{2,1},{3,2},{4,3},{5,4},{6,5},{7,6},{8,7},{9,8},{10,9},{11,1... | collective-permute-start | bytes 73736 | tf_op jit(solution)/shard_map/ppermute | solution.py:103
  93.4 1.6 collective-permute-done.2
  95.0 4.4 %collective-permute-start.10 = (bf16[8,12,128]{2,1,0:T(8,128)(2,1)S(1)}, bf16[8,12,128]{2,1,0:T(8,128)(2,1)S(1)}, u32[]{:S(2)}, u32[]{:S(2)}) collective-permute-start(bf16[8,12,128]{2,1,0:T(8,128)(2,1)S(1)} %collective-permute-done.9), channel_id=1, source_target_pairs={{1,0},{2,1},{3,2},{4,3},{5,4},{6,5},{7,6},{8,7},{9,8},{10,9},{11,1... | collective-permute-start | bytes 73736 | tf_op jit(solution)/shard_map/ppermute | solution.py:103
  99.4 1.6 collective-permute-done.3
  101.0 4.4 %collective-permute-start.11 = (bf16[8,12,128]{2,1,0:T(8,128)(2,1)S(1)}, bf16[8,12,128]{2,1,0:T(8,128)(2,1)S(1)}, u32[]{:S(2)}, u32[]{:S(2)}) collective-permute-start(bf16[8,12,128]{2,1,0:T(8,128)(2,1)S(1)} %collective-permute-done.10), channel_id=1, source_target_pairs={{1,0},{2,1},{3,2},{4,3},{5,4},{6,5},{7,6},{8,7},{9,8},{10,9},{11,1... | collective-permute-start | bytes 73736 | tf_op jit(solution)/shard_map/ppermute | solution.py:103
  105.4 1.6 collective-permute-done.4
  107.0 0.5 convolution_convert_fusion.6
  107.5 4.5 %collective-permute-start.12 = (bf16[8,12,128]{2,1,0:T(8,128)(2,1)S(1)}, bf16[8,12,128]{2,1,0:T(8,128)(2,1)S(1)}, u32[]{:S(2)}, u32[]{:S(2)}) collective-permute-start(bf16[8,12,128]{2,1,0:T(8,128)(2,1)S(1)} %collective-permute-done.11), channel_id=1, source_target_pairs={{1,0},{2,1},{3,2},{4,3},{5,4},{6,5},{7,6},{8,7},{9,8},{10,9},{11,1... | collective-permute-start | bytes 73736 | tf_op jit(solution)/shard_map/ppermute | solution.py:103
  112.0 1.0 collective-permute-done.5
  113.1 0.5 collective-permute-done.12
  113.6 4.4 %collective-permute-start.13 = (bf16[8,12,128]{2,1,0:T(8,128)(2,1)S(1)}, bf16[8,12,128]{2,1,0:T(8,128)(2,1)S(1)}, u32[]{:S(2)}, u32[]{:S(2)}) collective-permute-start(bf16[8,12,128]{2,1,0:T(8,128)(2,1)S(1)} %collective-permute-done.12), channel_id=1, source_target_pairs={{1,0},{2,1},{3,2},{4,3},{5,4},{6,5},{7,6},{8,7},{9,8},{10,9},{11,1... | collective-permute-start | bytes 73736 | tf_op jit(solution)/shard_map/ppermute | solution.py:103
  118.1 1.0 collective-permute-done.6
  119.4 0.3 collective-permute-done.13
  119.7 4.4 %collective-permute-start.14 = (bf16[8,12,128]{2,1,0:T(8,128)(2,1)S(1)}, bf16[8,12,128]{2,1,0:T(8,128)(2,1)S(1)}, u32[]{:S(2)}, u32[]{:S(2)}) collective-permute-start(bf16[8,12,128]{2,1,0:T(8,128)(2,1)S(1)} %collective-permute-done.13), channel_id=1, source_target_pairs={{1,0},{2,1},{3,2},{4,3},{5,4},{6,5},{7,6},{8,7},{9,8},{10,9},{11,1... | collective-permute-start | bytes 73736 | tf_op jit(solution)/shard_map/ppermute | solution.py:103
  124.1 1.0 collective-permute-done.7
  125.4 0.2 collective-permute-done.14
  125.7 0.6 gather_fusion
  126.4 0.4 fusion.9
  126.8 0.5 copy-done.1
  127.3 0.6 fusion.49
  128.4 1.2 copy.130
  129.5 5.8 %all-to-all-start = ((bf16[2,128,768]{2,0,1:T(2,128)(2,1)}), bf16[2,128,768]{2,0,1:T(2,128)(2,1)S(1)}, u32[]{:S(2)}, u32[]{:S(2)}) async-start(bf16[2,128,768]{2,0,1:T(2,128)(2,1)} %copy.130), calls=%async_computation.1 | async-start | bytes 786432 | tf_op jit(solution)/shard_map/all_to_all | solution.py:133
  135.5 12.0 %all-to-all-done = bf16[2,128,768]{2,0,1:T(2,128)(2,1)S(1)} async-done(((bf16[2,128,768]{2,0,1:T(2,128)(2,1)}), bf16[2,128,768]{2,0,1:T(2,128)(2,1)S(1)}, u32[]{:S(2)}, u32[]{:S(2)}) %all-to-all-start) | async-done | bytes 393248 | tf_op jit(solution)/shard_map/all_to_all | solution.py:133
  147.6 1.7 convolution_convert_fusion.2
  149.4 1.6 reshape_reshape.15
  151.0 1.7 convolution_convert_fusion.1
  152.7 1.6 reshape_reshape.16
  154.3 1.7 convolution_convert_fusion.3
  156.0 1.6 reshape_reshape.14
  157.6 4.2 %fusion.50 = (f32[8,12,32]{2,1,0:T(8,128)S(1)}, f32[8,12,32,32]{2,3,1,0:T(8,128)}) fusion(bf16[32,8,12,64]{3,2,1,0:T(8,128)(2,1)} %reshape_reshape.16, bf16[32,8,12,64]{3,2,1,0:T(8,128)(2,1)} %reshape_reshape.15, pred[8,32]{1,0:T(8,128)(4,1)S(1)} %iota_compare_fusion), kind=kOutput, calls=%fused_computation.97 | convolution fusion | flops 12976159 | bytes 1192192 | tf_op jit(solution)/shard_map/sub | solution.py:146
  161.9 2.1 %fusion.5 = bf16[32,8,12,64]{3,0,2,1:T(8,128)(2,1)S(1)} fusion(f32[8,12,32,32]{2,3,1,0:T(8,128)} %get-tuple-element.10, bf16[32,8,12,64]{3,2,1,0:T(8,128)(2,1)S(1)} %copy-done.4, f32[8,12,32]{2,1,0:T(8,128)S(1)} %get-tuple-element.9), kind=kOutput, calls=%fused_computation.9 | convolution fusion | flops 12976128 | bytes 1191936 | tf_op jit(solution)/shard_map/chrs,sche->rche/dot_general | solution.py:147
  164.0 0.3 copy.137
  164.4 0.6 reshape.197
  165.0 15.5 %all_to_all.30 = bf16[32,8,768]{2,1,0:T(8,128)(2,1)S(1)} all-to-all(bf16[32,8,768]{2,1,0:T(8,128)(2,1)S(1)} %reshape.197), channel_id=1, replica_groups=mesh['grp'=2,'seq'=16] {'seq'}, dimensions={0} | all-to-all | bytes 786432 | tf_op jit(solution)/shard_map/all_to_all | solution.py:151
  180.5 2.5 %fusion.8 = bf16[2,128,768]{2,1,0:T(8,128)(2,1)} fusion(f32[2,128,768]{2,1,0:T(8,128)S(1)} %get-tuple-element.8, bf16[768,768]{1,0:T(8,128)(2,1)} %param.25, bf16[2,16,8,768]{3,2,0,1:T(8,128)(2,1)S(1)} %bitcast.92), kind=kOutput, calls=%fused_computation.15 | convolution fusion | flops 302383104 | bytes 2752512 | tf_op jit(solution)/shard_map/dot_general | solution.py:152
  (70 shorter events, 2.3 us)
Async XLA Ops:
  6.5 120.2 %copy-start = (bf16[768,768]{1,0:T(8,128)(2,1)S(1)}, bf16[768,768]{1,0:T(8,128)(2,1)}, u32[]{:S(2)}) copy-start(bf16[768,768]{1,0:T(8,128)(2,1)} %param.20) | copy-start | bytes 3538948
  6.5 3.8 %copy-start.2 = (bf16[768,768]{1,0:T(8,128)(2,1)S(1)}, bf16[768,768]{1,0:T(8,128)(2,1)}, u32[]{:S(2)}) copy-start(bf16[768,768]{1,0:T(8,128)(2,1)} %param.18) | copy-start | bytes 3538948
  6.5 69.2 %reduce-scatter.2.cloned.1.call-start = ((), (), s32[]{:S(2)}) async-start(), calls=%async_computation.3 | async-start | bytes 1114112 | tf_op jit(solution)/shard_map/reduce_scatter | solution.py:77
  12.8 0.7 copy-start.6
  12.9 0.7 copy-start.7
  14.1 93.0 %copy-start.3 = (bf16[768,768]{1,0:T(8,128)(2,1)S(1)}, bf16[768,768]{1,0:T(8,128)(2,1)}, u32[]{:S(2)}) copy-start(bf16[768,768]{1,0:T(8,128)(2,1)} %param.19) | copy-start | bytes 3538948
  76.8 6.1 %collective-permute-start = (bf16[8,12,128]{2,1,0:T(8,128)(2,1)S(1)}, bf16[8,12,128]{2,1,0:T(8,128)(2,1)S(1)}, u32[]{:S(2)}, u32[]{:S(2)}) collective-permute-start(bf16[8,12,128]{2,1,0:T(8,128)(2,1)S(1)} %fusion.15), channel_id=1, source_target_pairs={{0,1},{1,2},{2,3},{3,4},{4,5},{5,6},{6,7},{7,8},{8,9},{9,10},{10,1... | collective-permute-start | bytes 73736 | tf_op jit(solution)/shard_map/ppermute | solution.py:98
  82.9 6.0 %collective-permute-start.1 = (bf16[8,12,128]{2,1,0:T(8,128)(2,1)S(1)}, bf16[8,12,128]{2,1,0:T(8,128)(2,1)S(1)}, u32[]{:S(2)}, u32[]{:S(2)}) collective-permute-start(bf16[8,12,128]{2,1,0:T(8,128)(2,1)S(1)} %collective-permute-done), channel_id=1, source_target_pairs={{0,1},{1,2},{2,3},{3,4},{4,5},{5,6},{6,7},{7,8},{8,9},{9,10},{10,1... | collective-permute-start | bytes 73736 | tf_op jit(solution)/shard_map/ppermute | solution.py:98
  82.9 6.0 %collective-permute-start.8 = (bf16[8,12,128]{2,1,0:T(8,128)(2,1)S(1)}, bf16[8,12,128]{2,1,0:T(8,128)(2,1)S(1)}, u32[]{:S(2)}, u32[]{:S(2)}) collective-permute-start(bf16[8,12,128]{2,1,0:T(8,128)(2,1)S(1)} %fusion.15), channel_id=1, source_target_pairs={{1,0},{2,1},{3,2},{4,3},{5,4},{6,5},{7,6},{8,7},{9,8},{10,9},{11,1... | collective-permute-start | bytes 73736 | tf_op jit(solution)/shard_map/ppermute | solution.py:103
  88.9 6.0 %collective-permute-start.2 = (bf16[8,12,128]{2,1,0:T(8,128)(2,1)S(1)}, bf16[8,12,128]{2,1,0:T(8,128)(2,1)S(1)}, u32[]{:S(2)}, u32[]{:S(2)}) collective-permute-start(bf16[8,12,128]{2,1,0:T(8,128)(2,1)S(1)} %collective-permute-done.1), channel_id=1, source_target_pairs={{0,1},{1,2},{2,3},{3,4},{4,5},{5,6},{6,7},{7,8},{8,9},{9,10},{10,1... | collective-permute-start | bytes 73736 | tf_op jit(solution)/shard_map/ppermute | solution.py:98
  88.9 6.0 %collective-permute-start.9 = (bf16[8,12,128]{2,1,0:T(8,128)(2,1)S(1)}, bf16[8,12,128]{2,1,0:T(8,128)(2,1)S(1)}, u32[]{:S(2)}, u32[]{:S(2)}) collective-permute-start(bf16[8,12,128]{2,1,0:T(8,128)(2,1)S(1)} %collective-permute-done.8), channel_id=1, source_target_pairs={{1,0},{2,1},{3,2},{4,3},{5,4},{6,5},{7,6},{8,7},{9,8},{10,9},{11,1... | collective-permute-start | bytes 73736 | tf_op jit(solution)/shard_map/ppermute | solution.py:103
  95.0 6.0 %collective-permute-start.3 = (bf16[8,12,128]{2,1,0:T(8,128)(2,1)S(1)}, bf16[8,12,128]{2,1,0:T(8,128)(2,1)S(1)}, u32[]{:S(2)}, u32[]{:S(2)}) collective-permute-start(bf16[8,12,128]{2,1,0:T(8,128)(2,1)S(1)} %collective-permute-done.2), channel_id=1, source_target_pairs={{0,1},{1,2},{2,3},{3,4},{4,5},{5,6},{6,7},{7,8},{8,9},{9,10},{10,1... | collective-permute-start | bytes 73736 | tf_op jit(solution)/shard_map/ppermute | solution.py:98
  95.0 6.0 %collective-permute-start.10 = (bf16[8,12,128]{2,1,0:T(8,128)(2,1)S(1)}, bf16[8,12,128]{2,1,0:T(8,128)(2,1)S(1)}, u32[]{:S(2)}, u32[]{:S(2)}) collective-permute-start(bf16[8,12,128]{2,1,0:T(8,128)(2,1)S(1)} %collective-permute-done.9), channel_id=1, source_target_pairs={{1,0},{2,1},{3,2},{4,3},{5,4},{6,5},{7,6},{8,7},{9,8},{10,9},{11,1... | collective-permute-start | bytes 73736 | tf_op jit(solution)/shard_map/ppermute | solution.py:103
  101.0 6.0 %collective-permute-start.4 = (bf16[8,12,128]{2,1,0:T(8,128)(2,1)S(1)}, bf16[8,12,128]{2,1,0:T(8,128)(2,1)S(1)}, u32[]{:S(2)}, u32[]{:S(2)}) collective-permute-start(bf16[8,12,128]{2,1,0:T(8,128)(2,1)S(1)} %collective-permute-done.3), channel_id=1, source_target_pairs={{0,1},{1,2},{2,3},{3,4},{4,5},{5,6},{6,7},{7,8},{8,9},{9,10},{10,1... | collective-permute-start | bytes 73736 | tf_op jit(solution)/shard_map/ppermute | solution.py:98
  101.0 6.5 %collective-permute-start.11 = (bf16[8,12,128]{2,1,0:T(8,128)(2,1)S(1)}, bf16[8,12,128]{2,1,0:T(8,128)(2,1)S(1)}, u32[]{:S(2)}, u32[]{:S(2)}) collective-permute-start(bf16[8,12,128]{2,1,0:T(8,128)(2,1)S(1)} %collective-permute-done.10), channel_id=1, source_target_pairs={{1,0},{2,1},{3,2},{4,3},{5,4},{6,5},{7,6},{8,7},{9,8},{10,9},{11,1... | collective-permute-start | bytes 73736 | tf_op jit(solution)/shard_map/ppermute | solution.py:103
  107.0 6.0 %collective-permute-start.5 = (bf16[8,12,128]{2,1,0:T(8,128)(2,1)S(1)}, bf16[8,12,128]{2,1,0:T(8,128)(2,1)S(1)}, u32[]{:S(2)}, u32[]{:S(2)}) collective-permute-start(bf16[8,12,128]{2,1,0:T(8,128)(2,1)S(1)} %collective-permute-done.4), channel_id=1, source_target_pairs={{0,1},{1,2},{2,3},{3,4},{4,5},{5,6},{6,7},{7,8},{8,9},{9,10},{10,1... | collective-permute-start | bytes 73736 | tf_op jit(solution)/shard_map/ppermute | solution.py:98
  107.5 6.1 %collective-permute-start.12 = (bf16[8,12,128]{2,1,0:T(8,128)(2,1)S(1)}, bf16[8,12,128]{2,1,0:T(8,128)(2,1)S(1)}, u32[]{:S(2)}, u32[]{:S(2)}) collective-permute-start(bf16[8,12,128]{2,1,0:T(8,128)(2,1)S(1)} %collective-permute-done.11), channel_id=1, source_target_pairs={{1,0},{2,1},{3,2},{4,3},{5,4},{6,5},{7,6},{8,7},{9,8},{10,9},{11,1... | collective-permute-start | bytes 73736 | tf_op jit(solution)/shard_map/ppermute | solution.py:103
  113.1 6.0 %collective-permute-start.6 = (bf16[8,12,128]{2,1,0:T(8,128)(2,1)S(1)}, bf16[8,12,128]{2,1,0:T(8,128)(2,1)S(1)}, u32[]{:S(2)}, u32[]{:S(2)}) collective-permute-start(bf16[8,12,128]{2,1,0:T(8,128)(2,1)S(1)} %collective-permute-done.5), channel_id=1, source_target_pairs={{0,1},{1,2},{2,3},{3,4},{4,5},{5,6},{6,7},{7,8},{8,9},{9,10},{10,1... | collective-permute-start | bytes 73736 | tf_op jit(solution)/shard_map/ppermute | solution.py:98
  113.6 6.0 %collective-permute-start.13 = (bf16[8,12,128]{2,1,0:T(8,128)(2,1)S(1)}, bf16[8,12,128]{2,1,0:T(8,128)(2,1)S(1)}, u32[]{:S(2)}, u32[]{:S(2)}) collective-permute-start(bf16[8,12,128]{2,1,0:T(8,128)(2,1)S(1)} %collective-permute-done.12), channel_id=1, source_target_pairs={{1,0},{2,1},{3,2},{4,3},{5,4},{6,5},{7,6},{8,7},{9,8},{10,9},{11,1... | collective-permute-start | bytes 73736 | tf_op jit(solution)/shard_map/ppermute | solution.py:103
  119.1 6.0 %collective-permute-start.7 = (bf16[8,12,128]{2,1,0:T(8,128)(2,1)S(1)}, bf16[8,12,128]{2,1,0:T(8,128)(2,1)S(1)}, u32[]{:S(2)}, u32[]{:S(2)}) collective-permute-start(bf16[8,12,128]{2,1,0:T(8,128)(2,1)S(1)} %collective-permute-done.6), channel_id=1, source_target_pairs={{0,1},{1,2},{2,3},{3,4},{4,5},{5,6},{6,7},{7,8},{8,9},{9,10},{10,1... | collective-permute-start | bytes 73736 | tf_op jit(solution)/shard_map/ppermute | solution.py:98
  119.7 6.0 %collective-permute-start.14 = (bf16[8,12,128]{2,1,0:T(8,128)(2,1)S(1)}, bf16[8,12,128]{2,1,0:T(8,128)(2,1)S(1)}, u32[]{:S(2)}, u32[]{:S(2)}) collective-permute-start(bf16[8,12,128]{2,1,0:T(8,128)(2,1)S(1)} %collective-permute-done.13), channel_id=1, source_target_pairs={{1,0},{2,1},{3,2},{4,3},{5,4},{6,5},{7,6},{8,7},{9,8},{10,9},{11,1... | collective-permute-start | bytes 73736 | tf_op jit(solution)/shard_map/ppermute | solution.py:103
  126.3 1.0 copy-start.1
  127.3 0.8 copy-start.5
  129.5 18.0 %all-to-all-start = ((bf16[2,128,768]{2,0,1:T(2,128)(2,1)}), bf16[2,128,768]{2,0,1:T(2,128)(2,1)S(1)}, u32[]{:S(2)}, u32[]{:S(2)}) async-start(bf16[2,128,768]{2,0,1:T(2,128)(2,1)} %copy.130), calls=%async_computation.1 | async-start | bytes 786432 | tf_op jit(solution)/shard_map/all_to_all | solution.py:133
  157.6 4.2 %copy-start.4 = (bf16[32,8,12,64]{3,2,1,0:T(8,128)(2,1)S(1)}, bf16[32,8,12,64]{3,2,1,0:T(8,128)(2,1)}, u32[]{:S(2)}) copy-start(bf16[32,8,12,64]{3,2,1,0:T(8,128)(2,1)} %reshape_reshape.14) | copy-start | bytes 1179652
Sparse Core Ops, SparseCore 0:
  15.6 60.1 reduce-scatter.1
